TPU v7x, 32 devices: a whole 2x2x4 slice. The times are simulated.
32 devices in a mesh: dp: 8 (over z, x), latent: 4 (over y, core).
Axes of the slice: x: 2, y: 2, z: 4, core: 2. Of those that a mesh axis runs over, the one named last changes fastest.
Arguments:
- tokens: bfloat16 [1024, 1536], P('dp'), may hold values from -6 to 6
- enc_weight: bfloat16 [1536, 32768], P(None, ('dp', 'latent')), may hold values from -0.15625 to 0.15625
- enc_bias: float32 [32768], P(('dp', 'latent')), may hold values from -3 to 3
- dec_weight: bfloat16 [32768, 1536], P(('dp', 'latent')), may hold values from -0.0625 to 0.0625
- dec_bias: float32 [1536], replicated, may hold values from -3 to 3
- slot_token: int32 [1024], P(('dp', 'latent')), may hold values from 0 to 7
- slot_latent: int32 [1024], P(('dp', 'latent')), may hold values from 0 to 7
- slot_count: int32 [32], P(('dp', 'latent')), may hold values from 6 to 32, as said below
Outputs:
- enc_grad: bfloat16 [1536, 32768], P(None, ('dp', 'latent'))
- dec_grad: bfloat16 [32768, 1536], P(('dp', 'latent'))
- enc_bias_grad: float32 [32768], P(('dp', 'latent'))
- dec_bias_grad: float32 [1536], replicated
- mean_error: float32 [], replicated
Inputs may be any that keep to these rules, and one draw needn't show every extreme that they name: `slot_count`: slot lists of one device never repeat a (token block, latent block) pair among its 32 slots; entries past a device's count name valid blocks and are ignored; some device has all 32 slots live in every draw.
All inputs are finite; a program needn't handle non-finite values.
Results may differ from a plain program's by a relative error of at most 0.0065.
Values may be sent and summed in bfloat16 or wider, within the bound.
A program may use at most 128 MiB of HBM per device.

v0:
```python
import jax
import jax.numpy as jnp
from jax import lax
from jax.sharding import PartitionSpec as P

BLK = 128


def local(tokens, enc_weight, enc_bias, dec_weight, dec_bias, slot_token, slot_latent, slot_count):
    block_size = BLK
    gathered = lax.all_gather(tokens, "dp", axis=0, tiled=True)
    total_rows = gathered.shape[0]
    features = tokens.shape[1]
    capacity = slot_token.shape[0]
    live_count = slot_count[0]

    def forward_slot(slot_index, carried):
        activations, partial_value = carried
        row_start = slot_token[slot_index] * block_size
        col_start = slot_latent[slot_index] * block_size
        tok_rows = lax.dynamic_slice_in_dim(gathered, row_start, block_size, 0)
        enc_block = lax.dynamic_slice_in_dim(enc_weight, col_start, block_size, 1)
        bias_block = lax.dynamic_slice_in_dim(enc_bias, col_start, block_size, 0)
        active = (
            jnp.dot(tok_rows, enc_block, preferred_element_type=jnp.float32) + bias_block[None, :]
        ).astype(jnp.bfloat16)
        dec_block = lax.dynamic_slice_in_dim(dec_weight, col_start, block_size, 0)
        contrib = jnp.dot(active, dec_block, preferred_element_type=jnp.float32)
        previous = lax.dynamic_slice_in_dim(partial_value, row_start, block_size, 0)
        partial_value = lax.dynamic_update_slice_in_dim(
            partial_value, previous + contrib, row_start, 0
        )
        activations = lax.dynamic_update_index_in_dim(activations, active, slot_index, 0)
        return (activations, partial_value)

    empty_acts = jnp.zeros((capacity, block_size, block_size), jnp.bfloat16)
    empty_sum = jnp.zeros((total_rows, features), jnp.float32)
    activations, partial_value = lax.fori_loop(0, live_count, forward_slot, (empty_acts, empty_sum))
    share = lax.psum_scatter(partial_value, ("dp", "latent"), scatter_dimension=0, tiled=True)
    share_rows = share.shape[0]
    offset = lax.axis_index("latent") * share_rows
    token_share = lax.dynamic_slice_in_dim(tokens, offset, share_rows, 0)
    residual = share + dec_bias[None, :] - token_share.astype(jnp.float32)
    scaled = residual * 0.25
    squared, dec_bias_grad = lax.psum(
        (jnp.sum(residual * residual), jnp.sum(scaled, axis=0)), ("dp", "latent")
    )
    grad_all = lax.all_gather(scaled.astype(jnp.bfloat16), ("dp", "latent"), axis=0, tiled=True)
    mean_error = squared / (total_rows * features)

    def backward_slot(slot_index, gradients):
        enc_acc, dec_acc, bias_acc = gradients
        row_start = slot_token[slot_index] * block_size
        col_start = slot_latent[slot_index] * block_size
        tok_rows = lax.dynamic_slice_in_dim(gathered, row_start, block_size, 0)
        grad_block = lax.dynamic_slice_in_dim(grad_all, row_start, block_size, 0)
        dec_block = lax.dynamic_slice_in_dim(dec_weight, col_start, block_size, 0)
        pre_grad = lax.dot_general(
            grad_block, dec_block, (((1,), (1,)), ((), ())), preferred_element_type=jnp.float32
        )
        old_bias = lax.dynamic_slice_in_dim(bias_acc, col_start, block_size, 0)
        bias_acc = lax.dynamic_update_slice_in_dim(
            bias_acc, old_bias + jnp.sum(pre_grad, axis=0), col_start, 0
        )
        pre_half = pre_grad.astype(jnp.bfloat16)
        enc_term = lax.dot_general(
            tok_rows, pre_half, (((0,), (0,)), ((), ())), preferred_element_type=jnp.float32
        )
        old_enc = lax.dynamic_slice_in_dim(enc_acc, col_start, block_size, 1)
        enc_acc = lax.dynamic_update_slice_in_dim(enc_acc, old_enc + enc_term, col_start, 1)
        dec_term = lax.dot_general(
            activations[slot_index],
            grad_block,
            (((0,), (0,)), ((), ())),
            preferred_element_type=jnp.float32,
        )
        old_dec = lax.dynamic_slice_in_dim(dec_acc, col_start, block_size, 0)
        dec_acc = lax.dynamic_update_slice_in_dim(dec_acc, old_dec + dec_term, col_start, 0)
        return (enc_acc, dec_acc, bias_acc)

    latents_here = enc_weight.shape[1]
    start_grads = (
        jnp.zeros((features, latents_here), jnp.float32),
        jnp.zeros((latents_here, features), jnp.float32),
        jnp.zeros((latents_here,), jnp.float32),
    )
    enc_acc, dec_acc, bias_acc = lax.fori_loop(0, live_count, backward_slot, start_grads)
    return (
        enc_acc.astype(jnp.bfloat16),
        dec_acc.astype(jnp.bfloat16),
        bias_acc,
        dec_bias_grad,
        mean_error,
    )


def solution(mesh):
    in_specs = (
        P("dp", None),
        P(None, ("dp", "latent")),
        P(("dp", "latent")),
        P(("dp", "latent"), None),
        P(),
        P(("dp", "latent")),
        P(("dp", "latent")),
        P(("dp", "latent")),
    )
    out_specs = (
        P(None, ("dp", "latent")),
        P(("dp", "latent"), None),
        P(("dp", "latent")),
        P(),
        P(),
    )
    return jax.shard_map(local, mesh=mesh, in_specs=in_specs, out_specs=out_specs, check_vma=False)
```

profile of v0, /device:TPU:7, one launch (start us, length us, event | category | flops | bytes accessed | tf_op | source)
XLA Modules:
  0.0 829.1 jit_solution(1080155368049432398)
XLA Ops:
  8.0 60.8 %all-gather.3.cloned.1.call-done = bf16[1024,1536]{1,0:T(8,128)(2,1)} async-done(((bf16[128,1536]{1,0:T(8,128)(2,1)}), bf16[1024,1536]{1,0:T(8,128)(2,1)}) %all-gather.3.cloned.1.call-update) | async-done | bytes 3145744 | tf_op jit(solution)/shard_map/all_gather | solution.py:11
  69.0 3.4 broadcast.5.clone
  72.4 247.6 %while.26 = (s32[]{:T(128)}, bf16[32,128,128]{2,1,0:T(8,128)(2,1)S(1)}, f32[1024,1536]{1,0:T(8,128)}, s32[]{:T(128)}, s32[32]{0:T(128)S(1)}, /*index=5*/bf16[102...) while((s32[]{:T(128)}, ...), condition=%wide.region_1.2_spmd, body=%wide.region_0.1_spmd.sunk | while | flops 100892688 | bytes 2852675 | solution.py:38
  320.1 114.0 %reduce-scatter.2.cloned.1.call-done = f32[32,1536]{1,0:T(8,128)} async-done(((f32[1024,1536]{1,0:T(8,128)}), f32[32,1536]{1,0:T(8,128)}) %reduce-scatter.2.cloned.1.call-update) | async-done | bytes 196624 | tf_op jit(solution)/shard_map/reduce_scatter | solution.py:39
  436.3 41.5 %all-reduce = (f32[1536]{0:T(1024)}, f32[]{:T(128)}) all-reduce(f32[1536]{0:T(1024)S(1)} %get-tuple-element.125, f32[]{:T(128)} %get-tuple-element.124), channel_id=1, replica_groups=mesh['dp'=8,'latent'=4] {'dp','latent'}, use_global_device_ids=true, to_apply=%region_7.8 | all-reduce | flops 1537 | bytes 12296 | tf_op jit(solution)/shard_map/psum | solution.py:45
  478.5 18.6 %all-gather.5.cloned.1.call-done = bf16[1024,1536]{1,0:T(8,128)(2,1)} async-done(((bf16[32,1536]{1,0:T(8,128)(2,1)}), bf16[1024,1536]{1,0:T(8,128)(2,1)}) %all-gather.5.cloned.1.call-update) | async-done | bytes 3145744 | tf_op jit(solution)/shard_map/all_gather | solution.py:48
  497.2 3.4 broadcast.5
  500.6 3.4 broadcast_in_dim.15
  504.0 310.2 %while.27 = (s32[]{:T(128)}, f32[1536,1024]{1,0:T(8,128)}, f32[1024,1536]{1,0:T(8,128)}, f32[1024]{0:T(1024)S(1)}, s32[]{:T(128)}, /*index=5*/s32[32]{0:T(128)S(...) while((s32[]{:T(128)}, f32[1536,1024]{1,0:T(8,128)}, ...), condition=%wide.region_5.6_spmd, body=%wide.region_3.0_spmd.sunk | while | flops 151420944 | bytes 4819283 | solution.py:87
  508.8 2.5 fusion.41
  511.3 2.5 fusion.42
  518.5 2.5 fusion.41
  528.2 2.5 fusion.41
  537.9 2.5 fusion.41
  540.4 2.4 fusion.42
  547.5 2.5 fusion.41
  550.0 2.5 fusion.42
  557.3 2.5 fusion.41
  559.8 2.5 fusion.42
  567.0 2.5 fusion.41
  569.5 2.4 fusion.42
  576.7 2.5 fusion.41
  579.2 2.5 fusion.42
  586.4 2.5 fusion.41
  588.8 2.5 fusion.42
  596.0 2.5 fusion.41
  598.5 2.5 fusion.42
  605.7 2.5 fusion.41
  608.2 2.4 fusion.42
  615.4 2.5 fusion.41
  617.8 2.5 fusion.42
  625.0 2.5 fusion.41
  627.5 2.5 fusion.42
  634.7 2.5 fusion.41
  644.3 2.5 fusion.41
  654.0 2.5 fusion.41
  656.5 2.4 fusion.42
  663.6 2.5 fusion.41
  673.3 2.5 fusion.41
  675.8 2.5 fusion.42
  683.0 2.5 fusion.41
  685.4 2.5 fusion.42
  692.6 2.5 fusion.41
  695.1 2.5 fusion.42
  702.4 2.5 fusion.41
  712.0 2.5 fusion.41
  714.5 2.5 fusion.42
  721.7 2.5 fusion.41
  724.1 2.5 fusion.42
  731.4 2.5 fusion.41
  733.9 2.5 fusion.42
  741.1 2.5 fusion.41
  750.7 2.5 fusion.41
  760.4 2.5 fusion.41
  762.9 2.5 fusion.42
  770.1 2.5 fusion.41
  772.5 2.5 fusion.42
  779.7 2.5 fusion.41
  789.4 2.5 fusion.41
  799.0 2.5 fusion.41
  801.5 2.5 fusion.42
  808.7 2.5 fusion.41
  811.1 2.5 fusion.42
  814.3 5.1 convert_element_type.20
  (318 shorter events, 301.2 us)
Async XLA Ops:
  7.2 65.2 %copy-start.3 = (s32[32]{0:T(128)S(1)}, s32[32]{0:T(128)}, u32[]{:S(2)}) copy-start(s32[32]{0:T(128)} %param.18) | copy-start | bytes 388
  7.2 65.2 %copy-start.4 = (s32[32]{0:T(128)S(1)}, s32[32]{0:T(128)}, u32[]{:S(2)}) copy-start(s32[32]{0:T(128)} %param.17) | copy-start | bytes 388
  7.2 61.5 %all-gather.3.cloned.1.call-start = ((), (), s32[]{:S(2)}) async-start(), calls=%async_computation.1 | async-start | bytes 3538944 | tf_op jit(solution)/shard_map/all_gather | solution.py:11
  7.9 426.1 %reduce-scatter.2.cloned.1.call-start = ((), (), s32[]{:S(2)}) async-start(), calls=%async_computation.2 | async-start | bytes 6488064 | tf_op jit(solution)/shard_map/reduce_scatter | solution.py:39
  320.0 114.1 %copy-start.2 = (f32[1536]{0:T(1024)S(1)}, f32[1536]{0:T(1024)}, u32[]{:S(2)}) copy-start(f32[1536]{0:T(1024)} %param.16) | copy-start | bytes 18436
  320.0 177.2 %all-gather.5.cloned.1.call-start = ((), (), s32[]{:S(2)}) async-start(), calls=%async_computation.3 | async-start | bytes 3244032 | tf_op jit(solution)/shard_map/all_gather | solution.py:48
  814.2 7.2 copy-start.1
  814.3 5.1 copy-start
Sparse Core Ops, SparseCore 0:
  10.2 58.5 all-gather.2
  320.1 113.8 reduce-scatter.1
  437.5 59.6 all-gather.4
where the time goes:
time: 836 us; the launch traced here: 829 us
  matrix products  324 us (39%)
  waiting for transfers between devices  194 us (23%)
  loops' own time  128 us (15%)
  local copies, waits for them, and re-layouts  110 us (13%)
  blocking collectives  41.5 us (5%)
  between operations  15.6 us (2%)
  other arithmetic  15.4 us (2%)
    reduce_scatter x1, waiting for transfers between devices, local(): lax.psum_scatter(partial_value, ('dp', 'latent'), scatter_dimension=0, ti...  114 us
    dot_general x32, matrix products, backward_slot(): lax.dot_general(tok_rows, pre_half, (((0,), (0,)), ((), ())), preferred_e...  79.5 us
    dot_general x32, matrix products, backward_slot(): lax.dot_general(activations[slot_index], grad_block, (((0,), (0,)), ((),...  78.3 us
    dot_general x32, matrix products, forward_slot(): contrib = jnp.dot(active, dec_block, preferred_element_type=jnp.float32)  77.1 us
    another operation x1, loops' own time, local(): lax.fori_loop(0, live_count, backward_slot, start_grads)  64.1 us
    another operation x1, loops' own time, local(): lax.fori_loop(0, live_count, forward_slot, (empty_acts, empty_sum))  64.1 us
    all_gather x1, waiting for transfers between devices, local(): gathered = lax.all_gather(tokens, 'dp', axis=0, tiled=True)  60.8 us
    dot_general x32, matrix products, backward_slot(): lax.dot_general(grad_block, dec_block, (((1,), (1,)), ((), ())), preferre...  44.6 us
  transfers between devices with their start and end apart: 3, of which 3 were waited for; matrix products, arithmetic and copies ran while one was open for 0% of the time, Pallas kernels for 0%

commit v1 on v0

--- a/solution.py
+++ b/solution.py
@@ -6,9 +6,27 @@
 BLK = 128
 
 
+def assign_patch(raw, in_dim):
+    block_next = list(raw.shape[1:])
+    block_next[in_dim] *= raw.shape[0]
+    return jnp.moveaxis(raw, 0, in_dim).reshape(block_next)
+
+
+def step_on_chains(xx, device_axis):
+    finding = xx[None]
+    k_all = jax.lax.axis_size(device_axis)
+    for pp in range(k_all.bit_length() - 1):
+        p_next = 1 << pp
+        oldest = jax.lax.ppermute(finding, device_axis, [(dd, dd ^ p_next) for dd in range(k_all)])
+        g_now = jnp.stack([finding, oldest])
+        left_arr = jax.lax.axis_index(device_axis) >> pp & 1
+        finding = jnp.where(left_arr == 0, g_now, g_now[::-1]).reshape(-1, *xx.shape)
+    return finding
+
+
 def local(tokens, enc_weight, enc_bias, dec_weight, dec_bias, slot_token, slot_latent, slot_count):
     block_size = BLK
-    gathered = lax.all_gather(tokens, "dp", axis=0, tiled=True)
+    gathered = assign_patch(step_on_chains(tokens, "dp"), 0)
     total_rows = gathered.shape[0]
     features = tokens.shape[1]
     capacity = slot_token.shape[0]

time: 836 us -> 889 us (1.063)
  waiting for transfers between devices: 194 us -> 226 us
  matrix products: 324 us -> 336 us
    ppermute x0 -> x3, waiting for transfers between devices: none -> 93.8 us  [step_on_chains(): jax.lax.ppermute(finding, device_axis, [(dd, dd ^ p_next) for dd in range...]
    all_gather x1 -> x0, waiting for transfers between devices: 60.8 us -> none  [local(): gathered = lax.all_gather(tokens, 'dp', axis=0, tiled=True)]
    dot_general x32, matrix products: 44.2 us -> 59.7 us  [forward_slot(): jnp.dot(tok_rows, enc_block, preferred_element_type=jnp.float32)]
  transfers between devices with their start and end apart: 3 -> 5, of which waited for: 3 -> 5; matrix products, arithmetic and copies ran while one was open for 0% -> 0% of each run, Pallas kernels for 0% -> 0%
where the time goes in v1:
time: 889 us; the launch traced here: 881 us
  matrix products  336 us (38%)
  waiting for transfers between devices  226 us (25%)
  loops' own time  128 us (14%)
  local copies, waits for them, and re-layouts  111 us (12%)
  blocking collectives  41.6 us (5%)
  other arithmetic  17.9 us (2%)
  between operations  15.9 us (2%)
    reduce_scatter x1, waiting for transfers between devices, local(): lax.psum_scatter(partial_value, ('dp', 'latent'), scatter_dimension=0, ti...  113 us
    ppermute x3, waiting for transfers between devices, step_on_chains(): jax.lax.ppermute(finding, device_axis, [(dd, dd ^ p_next) for dd in range...  93.8 us
    dot_general x32, matrix products, backward_slot(): lax.dot_general(activations[slot_index], grad_block, (((0,), (0,)), ((),...  79.1 us
    dot_general x32, matrix products, forward_slot(): contrib = jnp.dot(active, dec_block, preferred_element_type=jnp.float32)  76.9 us
    dot_general x32, matrix products, backward_slot(): lax.dot_general(tok_rows, pre_half, (((0,), (0,)), ((), ())), preferred_e...  76 us
    another operation x1, loops' own time, local(): lax.fori_loop(0, live_count, backward_slot, start_grads)  64.1 us
    another operation x1, loops' own time, local(): lax.fori_loop(0, live_count, forward_slot, (empty_acts, empty_sum))  64.1 us
    dot_general x32, matrix products, forward_slot(): jnp.dot(tok_rows, enc_block, preferred_element_type=jnp.float32)  59.7 us
  transfers between devices with their start and end apart: 5, of which 5 were waited for; matrix products, arithmetic and copies ran while one was open for 0% of the time, Pallas kernels for 0%

profile of v1, /device:TPU:7, one launch (start us, length us, event | category | flops | bytes accessed | tf_op | source)
XLA Modules:
  0.0 881.0 jit_solution(8619268157678724345)
XLA Ops:
  7.5 10.0 %collective-permute-done = bf16[1,128,1536]{2,1,0:T(8,128)(2,1)S(1)} collective-permute-done((bf16[1,128,1536]{2,1,0:T(8,128)(2,1)}, bf16[1,128,1536]{2,1,0:T(8,128)(2,1)S(1)}, u32[]{:S(2)}, u32[]{:S(2)}) %collective-permute-start) | collective-permute-done | bytes 393248 | tf_op jit(solution)/shard_map/ppermute | solution.py:20
  20.1 16.3 %collective-permute-done.1 = bf16[2,128,1536]{2,1,0:T(8,128)(2,1)S(1)} collective-permute-done((bf16[2,128,1536]{2,1,0:T(8,128)(2,1)S(1)}, bf16[2,128,1536]{2,1,0:T(8,128)(2,1)S(1)}, u32[]{:S(2)}, u32[]{:S(2)}) %collective-permute-start.1) | collective-permute-done | bytes 786464 | tf_op jit(solution)/shard_map/ppermute | solution.py:20
  39.2 67.6 %collective-permute-done.2 = bf16[4,128,1536]{2,1,0:T(8,128)(2,1)S(1)} collective-permute-done((bf16[4,128,1536]{2,1,0:T(8,128)(2,1)S(1)}, bf16[4,128,1536]{2,1,0:T(8,128)(2,1)S(1)}, u32[]{:S(2)}, u32[]{:S(2)}) %collective-permute-start.2) | collective-permute-done | bytes 1572896 | tf_op jit(solution)/shard_map/ppermute | solution.py:20
  108.9 3.5 broadcast.5.clone
  112.4 262.7 %while.26 = (s32[]{:T(128)}, bf16[32,128,128]{2,1,0:T(8,128)(2,1)}, f32[1024,1536]{1,0:T(8,128)}, s32[]{:T(128)}, s32[32]{0:T(128)S(1)}, /*index=5*/bf16[1024,15...) while((s32[]{:T(128)}, bf16[32,128,128]{2,1,0:T(8,128)(2,1)}, ...), condition=%wide.region_1.2_spmd, body=%wide.region_0.1_spmd.sunk | while | flops 100892688 | bytes 2852675 | solution.py:56
  118.1 2.4 fusion.37
  126.3 2.4 fusion.37
  142.7 2.4 fusion.37
  150.9 2.4 fusion.37
  208.2 2.4 fusion.37
  216.4 2.4 fusion.37
  224.6 2.4 fusion.37
  232.8 2.4 fusion.37
  257.4 2.4 fusion.37
  265.6 2.4 fusion.37
  273.8 2.4 fusion.37
  282.0 2.4 fusion.37
  290.2 2.4 fusion.37
  298.3 2.4 fusion.37
  306.6 2.4 fusion.37
  322.9 2.4 fusion.37
  331.1 2.4 fusion.37
  347.5 2.4 fusion.37
  355.7 2.4 fusion.37
  372.1 2.4 fusion.37
  375.2 113.1 %reduce-scatter.2.cloned.1.call-done = f32[32,1536]{1,0:T(8,128)} async-done(((f32[1024,1536]{1,0:T(8,128)}), f32[32,1536]{1,0:T(8,128)}) %reduce-scatter.2.cloned.1.call-update) | async-done | bytes 196624 | tf_op jit(solution)/shard_map/reduce_scatter | solution.py:57
  490.6 41.6 %all-reduce = (f32[1536]{0:T(1024)}, f32[]{:T(128)}) all-reduce(f32[1536]{0:T(1024)S(1)} %get-tuple-element.125, f32[]{:T(128)} %get-tuple-element.124), channel_id=1, replica_groups=mesh['dp'=8,'latent'=4] {'dp','latent'}, use_global_device_ids=true, to_apply=%region_7.8 | all-reduce | flops 1537 | bytes 12296 | tf_op jit(solution)/shard_map/psum | solution.py:63
  532.8 18.6 %all-gather.2.cloned.1.call-done = bf16[1024,1536]{1,0:T(8,128)(2,1)} async-done(((bf16[32,1536]{1,0:T(8,128)(2,1)}), bf16[1024,1536]{1,0:T(8,128)(2,1)}) %all-gather.2.cloned.1.call-update) | async-done | bytes 3145744 | tf_op jit(solution)/shard_map/all_gather | solution.py:66
  551.5 3.4 broadcast.5
  554.9 3.5 broadcast_in_dim.18
  558.4 307.5 %while.27 = (s32[]{:T(128)}, f32[1536,1024]{1,0:T(8,128)}, f32[1024,1536]{1,0:T(8,128)}, f32[1024]{0:T(1024)S(1)}, s32[]{:T(128)}, /*index=5*/s32[32]{0:T(128)S(...) while((s32[]{:T(128)}, f32[1536,1024]{1,0:T(8,128)}, ...), condition=%wide.region_5.6_spmd, body=%wide.region_3.5_spmd.sunk | while | flops 151420944 | bytes 4819283 | solution.py:105
  565.4 2.5 fusion.44
  575.1 2.4 fusion.44
  584.6 2.5 fusion.44
  594.2 2.4 fusion.44
  603.7 2.5 fusion.44
  613.3 2.5 fusion.44
  622.9 2.4 fusion.44
  632.5 2.5 fusion.44
  642.1 2.5 fusion.44
  651.8 2.5 fusion.44
  661.3 2.5 fusion.44
  670.9 2.5 fusion.44
  680.6 2.5 fusion.44
  690.2 2.4 fusion.44
  699.7 2.4 fusion.44
  709.2 2.4 fusion.44
  718.8 2.5 fusion.44
  728.4 2.5 fusion.44
  738.0 2.5 fusion.44
  747.6 2.5 fusion.44
  757.2 2.4 fusion.44
  766.8 2.5 fusion.44
  776.4 2.5 fusion.44
  786.0 2.5 fusion.44
  795.6 2.4 fusion.44
  805.2 2.5 fusion.44
  814.8 2.5 fusion.44
  824.4 2.5 fusion.44
  834.0 2.4 fusion.44
  843.5 2.4 fusion.44
  853.1 2.5 fusion.44
  862.7 2.5 fusion.44
  865.9 5.1 convert_element_type.20
  (327 shorter events, 327.0 us)
Async XLA Ops:
  7.2 481.2 %reduce-scatter.2.cloned.1.call-start = ((), (), s32[]{:S(2)}) async-start(), calls=%async_computation.1 | async-start | bytes 6488064 | tf_op jit(solution)/shard_map/reduce_scatter | solution.py:57
  7.2 10.3 %collective-permute-start = (bf16[1,128,1536]{2,1,0:T(8,128)(2,1)}, bf16[1,128,1536]{2,1,0:T(8,128)(2,1)S(1)}, u32[]{:S(2)}, u32[]{:S(2)}) collective-permute-start(bf16[1,128,1536]{2,1,0:T(8,128)(2,1)} %bitcast.45), channel_id=1, source_target_pairs={{0,4},{4,0},{8,12},{12,8},{16,20},{20,16},{24,28},{28,24},{1,5},{5... | collective-permute-start | bytes 1179656 | tf_op jit(solution)/shard_map/ppermute | solution.py:20
  18.7 17.6 %collective-permute-start.1 = (bf16[2,128,1536]{2,1,0:T(8,128)(2,1)S(1)}, bf16[2,128,1536]{2,1,0:T(8,128)(2,1)S(1)}, u32[]{:S(2)}, u32[]{:S(2)}) collective-permute-start(bf16[2,128,1536]{2,1,0:T(8,128)(2,1)S(1)} %get-tuple-element.175), channel_id=1, source_target_pairs={{0,8},{4,12},{8,0},{12,4},{16,24},{20,28},{24,16},{28,20},{1,9},{5... | collective-permute-start | bytes 2359304 | tf_op jit(solution)/shard_map/ppermute | solution.py:20
  36.8 70.0 %collective-permute-start.2 = (bf16[4,128,1536]{2,1,0:T(8,128)(2,1)S(1)}, bf16[4,128,1536]{2,1,0:T(8,128)(2,1)S(1)}, u32[]{:S(2)}, u32[]{:S(2)}) collective-permute-start(bf16[4,128,1536]{2,1,0:T(8,128)(2,1)S(1)} %bitcast.41), channel_id=1, source_target_pairs={{0,16},{4,20},{8,24},{12,28},{16,0},{20,4},{24,8},{28,12},{1,17},{... | collective-permute-start | bytes 4718600 | tf_op jit(solution)/shard_map/ppermute | solution.py:20
  108.9 3.5 copy-start.3
  108.9 3.5 copy-start.4
  375.1 113.2 %copy-start.2 = (f32[1536]{0:T(1024)S(1)}, f32[1536]{0:T(1024)}, u32[]{:S(2)}) copy-start(f32[1536]{0:T(1024)} %param.16) | copy-start | bytes 18436
  375.2 176.3 %all-gather.2.cloned.1.call-start = ((), (), s32[]{:S(2)}) async-start(), calls=%async_computation.2 | async-start | bytes 3244032 | tf_op jit(solution)/shard_map/all_gather | solution.py:66
  865.8 5.1 copy-start.1
  865.9 5.1 copy-start
Sparse Core Ops, SparseCore 0:
  375.3 113.0 reduce-scatter.1
  491.8 59.6 all-gather.1
